TPU v7x, 32 devices: a whole 2x2x4 slice. The times are simulated.
32 devices in a mesh: seq: 8 (over z, x), hx: 4 (over y, core).
Axes of the slice: x: 2, y: 2, z: 4, core: 2. Of those that a mesh axis runs over, the one named last changes fastest.
Arguments:
- query: bfloat16 [8192, 8192], P('seq', 'hx'), may hold values from -6 to 6
- key_in: bfloat16 [8192, 8192], P('seq', 'hx'), may hold values from -6 to 6
- value: bfloat16 [8192, 8192], P('seq', 'hx'), may hold values from -6 to 6
- head_gain: float32 [8192], P('hx'), may hold values from 0.1 to 1.9
- out_weight: bfloat16 [8192, 6144], P('hx', 'seq'), may hold values from -0.0625 to 0.0625
- residual: bfloat16 [8192, 6144], P(('seq', 'hx')), may hold values from -6 to 6
Outputs:
- mixed: bfloat16 [8192, 6144], P(('seq', 'hx'))
All inputs are finite; a program needn't handle non-finite values.
Results may differ from a plain program's by a relative error of at most 0.014.
Values may be sent and summed in bfloat16 or wider, within the bound.
A program may use at most 128 MiB of HBM per device.

v0:
```python
import jax
import jax.numpy as jnp
from jax import lax
from jax.sharding import PartitionSpec as P

DH = 128


def entering(x, axis, combine, identity):
    size, position = (lax.axis_size(axis), lax.axis_index(axis))
    everything = lax.all_gather(x.astype(jnp.bfloat16), axis)
    start = jnp.broadcast_to(jnp.asarray(identity, x.dtype), x.shape)

    def turn(k, before):
        reached = k < position
        new = combine(before, everything[k].astype(x.dtype))
        return jnp.where(reached, new, before)

    return lax.fori_loop(0, size, turn, start)


def activate(array):
    return jax.nn.silu(array.astype(jnp.float32)).astype(jnp.bfloat16)


def per_device(query, key_in, value, head_gain, out_weight, residual):
    highest = lax.Precision.HIGHEST
    tokens_here, width = query.shape
    heads = width // DH
    q_act = activate(query).reshape(tokens_here, heads, DH)
    k_act = activate(key_in).reshape(tokens_here, heads, DH)
    v_heads = value.reshape(tokens_here, heads, DH)
    blocks = min(512, tokens_here)
    count = tokens_here // blocks
    rows = jnp.arange(blocks, dtype=jnp.int32)
    lower = rows[:, None] >= rows[None, :]
    running = jnp.zeros((heads, DH, DH), jnp.float32)
    pieces = []
    for index in range(count):
        q_part = q_act[index * blocks : (index + 1) * blocks]
        k_part = k_act[index * blocks : (index + 1) * blocks]
        v_part = v_heads[index * blocks : (index + 1) * blocks]
        scores = jnp.einsum("thd,shd->hts", q_part, k_part, preferred_element_type=jnp.float32)
        scores = jnp.where(lower[None, :, :], scores, jnp.zeros_like(scores))
        inner = jnp.einsum("hts,she->the", scores, v_part.astype(jnp.float32), precision=highest)
        if index > 0:
            inner = inner + jnp.einsum(
                "thd,hde->the", q_part.astype(jnp.float32), running, precision=highest
            )
        pieces.append(inner)
        running = running + jnp.einsum(
            "thd,the->hde", k_part, v_part, preferred_element_type=jnp.float32
        )
    local_part = jnp.concatenate(pieces, axis=0)
    empty = jnp.zeros((heads, DH, DH), jnp.float32)

    def combine(earlier, later):
        return earlier + later

    prefix = entering(running, "seq", combine, empty)
    attended = local_part + jnp.einsum(
        "thd,hde->the", q_act.astype(jnp.float32), prefix, precision=highest
    )
    meansq = jnp.mean(attended * attended, axis=-1, keepdims=True)
    normed = attended * lax.rsqrt(meansq + 1e-06) * head_gain.reshape(heads, DH)
    normed = normed.astype(jnp.bfloat16).reshape(tokens_here, width)
    full_weight = lax.all_gather(out_weight, "seq", axis=1, tiled=True)
    summed = lax.psum_scatter(
        jnp.dot(normed, full_weight, preferred_element_type=jnp.float32).astype(jnp.bfloat16),
        "hx",
        scatter_dimension=0,
        tiled=True,
    ).astype(jnp.float32)
    return (summed + residual.astype(jnp.float32)).astype(jnp.bfloat16)


def solution(mesh):
    return jax.shard_map(
        per_device,
        mesh=mesh,
        in_specs=(
            P("seq", "hx"),
            P("seq", "hx"),
            P("seq", "hx"),
            P("hx"),
            P("hx", "seq"),
            P(("seq", "hx"), None),
        ),
        out_specs=P(("seq", "hx"), None),
        check_vma=False,
    )
```

profile of v0, /device:TPU:0, one launch (start us, length us, event | category | flops | bytes accessed | tf_op | source)
XLA Modules:
  0.0 733.0 jit_solution(13041921529370957699)
XLA Ops:
  6.5 0.0 all-gather.6.cloned.1.call-start
  6.5 6.4 copy.48
  12.9 4.1 fusion.11
  17.0 0.0 copy-start.8
  17.0 2.4 fusion.24
  19.4 1.3 copy-done.8
  20.7 1.8 fusion.23
  22.5 2.5 copy.81
  25.0 2.9 copy.80
  27.9 0.0 copy-start.2
  27.9 0.0 copy-start.3
  27.9 2.4 fusion.27
  30.4 0.0 copy-start.6
  30.4 1.0 copy-done.6
  31.4 0.0 copy-done.2
  31.4 0.0 copy-done.3
  31.4 1.5 fusion.19
  32.9 0.0 all-gather.6.cloned.1.call-update
  32.9 0.0 all-gather.4.cloned.1.call-start
  33.0 0.7 all-gather.4.cloned.1.call-update
  33.7 0.2 reduce-scatter.2.cloned.1.call-start
  33.9 6.4 copy.47
  40.3 0.1 iota_compare_fusion
  40.4 4.1 fusion.7
  44.4 0.0 copy-start
  44.4 0.0 copy-start.4
  44.5 1.6 fusion.22
  46.1 1.2 copy-done
  47.2 0.0 copy-start.5
  47.2 1.3 copy-done.5
  48.6 0.0 copy-done.4
  48.6 2.4 fusion.26
  50.9 11.2 %fusion = f32[16,512,128]{2,1,0:T(8,128)} fusion(bf16[512,16,128]{0,2,1:T(8,128)(2,1)} %bitcast.44, f32[16,512,512]{2,1,0:T(8,128)S(1)} %fusion.26, pred[512,512]{1,0:T(8,128)(4,1)S(1)} %iota_compare_fusion), kind=kOutput, calls=%fused_computation.1 | convolution fusion | flops 6446645248 | bytes 23330816 | tf_op jit(solution)/shard_map/hts,she->the/dot_general | solution.py:45
  62.1 0.0 copy-start.1
  62.1 0.0 copy-start.7
  62.2 7.3 %bitcast_add_fusion = f32[512,16,128]{2,0,1:T(8,128)} fusion(f32[16,512,128]{2,1,0:T(8,128)} %fusion, f32[16,128,128]{2,1,0:T(8,128)} %copy-done.6, bf16[512,16,128]{0,2,1:T(8,128)(2,1)} %bitcast.49), kind=kOutput, calls=%fused_computation.26 | convolution fusion | flops 1611661312 | bytes 11534336 | tf_op jit(solution)/shard_map/thd,hde->the/dot_general | solution.py:47
  69.5 0.0 copy-done.1
  69.5 0.0 copy-done.7
  69.5 2.4 fusion.25
  71.9 10.0 %fusion.16 = f32[512,16,128]{2,0,1:T(8,128)} fusion(bf16[512,16,128]{0,2,1:T(8,128)(2,1)S(1)} %bitcast.41, f32[16,512,512]{2,1,0:T(8,128)S(1)} %fusion.25, pred[512,512]{1,0:T(8,128)(4,1)S(1)} %iota_compare_fusion), kind=kOutput, calls=%fused_computation.27 | convolution fusion | flops 6446645248 | bytes 23330816 | tf_op jit(solution)/shard_map/hts,she->the/dot_general | solution.py:45
  81.8 26.7 %all-gather.6.cloned.1.call-done = bf16[128,128,128]{2,1,0:T(8,128)(2,1)} async-done(((bf16[16,128,128]{2,1,0:T(8,128)(2,1)}), bf16[128,128,128]{2,1,0:T(8,128)(2,1)}) %all-gather.6.cloned.1.call-update) | async-done | bytes 4194320 | tf_op jit(solution)/shard_map/all_gather | solution.py:11
  108.6 13.2 %while.14 = (s32[]{:T(128)}, f32[16,128,128]{2,1,0:T(8,128)S(1)}, s32[]{:T(128)}, bf16[8,16,128,128]{3,2,1,0:T(8,128)(2,1)}, s32[]{:T(128)}, /*index=5*/s32[]{:T(128)}) while((s32[]{:T(128)}, f32[16,128,128]{2,1,0:T(8,128)S(1)}, s32[]{:T(128)}, bf16[8,16,128,128]{3,2,1,0:T(8,128)(2,1)}, s32[]{:T(128)}, /*index=5*/s32[]{:T(128)}) %tuple.45), condition=%wide.region_1.2_spmd.clone, body=%wide.region_0.1_spmd.clone.sunk | while | flops 1048580 | bytes 2621533 | solution.py:19
  108.6 1.6 add_select_fusion.2
  110.2 1.6 add_select_fusion.2
  111.9 1.6 add_select_fusion.2
  113.5 1.6 add_select_fusion.2
  115.1 1.7 add_select_fusion.2
  116.8 1.7 add_select_fusion.2
  118.5 1.6 add_select_fusion.2
  120.2 1.6 add_select_fusion.2
  121.8 0.0 copy-start.10
  121.8 11.0 %multiply_reduce_fusion = (f32[1024,16]{0,1:T(8,128)S(1)}, f32[1024,16,128]{2,0,1:T(8,128)}) fusion(f32[16,128,128]{2,1,0:T(8,128)S(1)} %get-tuple-element.84, bf16[1024,16,128]{0,2,1:T(8,128)(2,1)} %bitcast.39, f32[512,16,128]{2,0,1:T(8,128)} %bitcast_add_fusion, f32[512,16,128]{2,0,1:T(8,128)} %fusion.16), kind=kOutput, calls=%fused_computation.20 | convolution fusion | flops 3229597696 | bytes 22085632 | tf_op jit(solution)/shard_map/thd,hde->the/dot_general | solution.py:61
  132.8 0.0 copy-done.10
  132.8 6.9 multiply_convert_fusion
  139.7 6.4 copy.65
  146.1 442.9 %all-gather.4.cloned.1.call-done = bf16[2048,6144]{1,0:T(8,128)(2,1)} async-done(((bf16[2048,768]{1,0:T(8,128)(2,1)}), bf16[2048,6144]{1,0:T(8,128)(2,1)}) %all-gather.4.cloned.1.call-update) | async-done | bytes 25165840 | tf_op jit(solution)/shard_map/all_gather | solution.py:67
  589.1 32.9 %convolution_convert_fusion = bf16[1024,6144]{1,0:T(8,128)(2,1)} fusion(bf16[1024,2048]{0,1:T(8,128)(2,1)} %bitcast.51, bf16[2048,6144]{1,0:T(8,128)(2,1)} %all-gather.4.cloned.1.call-done), kind=kOutput, calls=%fused_computation.5 | convolution fusion | flops 25776095232 | bytes 41943040 | tf_op jit(solution)/shard_map/dot_general | solution.py:69
  622.0 0.0 copy-start.9
  622.0 0.0 reduce-scatter.2.cloned.1.call-update
  622.0 99.7 %reduce-scatter.2.cloned.1.call-done = bf16[256,6144]{1,0:T(8,128)(2,1)} async-done(((bf16[1024,6144]{1,0:T(8,128)(2,1)}), bf16[256,6144]{1,0:T(8,128)(2,1)}) %reduce-scatter.2.cloned.1.call-update) | async-done | bytes 3145744 | tf_op jit(solution)/shard_map/reduce_scatter | solution.py:68
  721.7 0.0 copy-done.9
  721.7 4.7 add_convert_fusion
  (2 shorter events, 0.0 us)
Async XLA Ops:
  6.5 102.1 %all-gather.6.cloned.1.call-start = ((), (), s32[]{:S(2)}) async-start(), calls=%async_computation.3 | async-start | bytes 4718592 | tf_op jit(solution)/shard_map/all_gather | solution.py:11
  17.0 3.7 copy-start.8
  27.9 3.5 copy-start.2
  27.9 3.5 copy-start.3
  30.4 1.0 copy-start.6
  32.9 556.1 %all-gather.4.cloned.1.call-start = ((), (), s32[]{:S(2)}) async-start(), calls=%async_computation.1 | async-start | bytes 28311552 | tf_op jit(solution)/shard_map/all_gather | solution.py:67
  33.7 688.1 %reduce-scatter.2.cloned.1.call-start = ((), (), s32[]{:S(2)}) async-start(), calls=%async_computation.2 | async-start | bytes 15728640 | tf_op jit(solution)/shard_map/reduce_scatter | solution.py:68
  44.4 2.8 copy-start
  44.4 4.1 copy-start.4
  47.2 1.3 copy-start.5
  62.1 7.4 %copy-start.1 = (bf16[512,2048]{0,1:T(8,128)(2,1)S(1)}, bf16[512,2048]{0,1:T(8,128)(2,1)}, u32[]{:S(2)}) copy-start(bf16[512,2048]{0,1:T(8,128)(2,1)} %get-tuple-element.112) | copy-start | bytes 6291460
  62.1 7.4 %copy-start.7 = (bf16[512,2048]{0,1:T(8,128)(2,1)S(1)}, bf16[512,2048]{0,1:T(8,128)(2,1)}, u32[]{:S(2)}) copy-start(bf16[512,2048]{0,1:T(8,128)(2,1)} %get-tuple-element.108) | copy-start | bytes 6291460
  121.8 11.0 %copy-start.10 = (f32[2048]{0:T(1024)S(1)}, f32[2048]{0:T(1024)}, u32[]{:S(2)}) copy-start(f32[2048]{0:T(1024)} %param.11) | copy-start | bytes 24580
  622.0 99.8 %copy-start.9 = (bf16[256,6144]{1,0:T(8,128)(2,1)S(1)}, bf16[256,6144]{1,0:T(8,128)(2,1)}, u32[]{:S(2)}) copy-start(bf16[256,6144]{1,0:T(8,128)(2,1)} %param.13) | copy-start | bytes 9437188
Sparse Core Ops, SparseCore 0:
  33.0 75.4 all-gather.5
  110.1 478.8 all-gather.3
  622.1 99.5 reduce-scatter.1
where the time goes:
time: 734 us; the launch traced here: 733 us
  waiting for transfers between devices  570 us (78%)
  matrix products  81.1 us (11%)
  local copies, waits for them, and re-layouts  35.2 us (5%)
  other arithmetic  32.9 us (4%)
  between operations  13.3 us (2%)
    all_gather x1, waiting for transfers between devices, per_device(): full_weight = lax.all_gather(out_weight, 'seq', axis=1, tiled=True)  443 us
    reduce_scatter x1, waiting for transfers between devices, per_device(): lax.psum_scatter(jnp.dot(normed, full_weight, preferred_element_type=jnp....  99.7 us
    dot_general x1, matrix products, per_device(): jnp.dot(normed, full_weight, preferred_element_type=jnp.float32)  32.9 us
    all_gather x1, waiting for transfers between devices, entering(): everything = lax.all_gather(x.astype(jnp.bfloat16), axis)  26.7 us
    unnamed x26, local copies, waits for them, and re-layouts  22.9 us
    dot_general x2, matrix products, per_device(): jnp.einsum('hts,she->the', scores, v_part.astype(jnp.float32), precision=...  21.2 us
  transfers between devices with their start and end apart: 3, of which 3 were waited for; matrix products, arithmetic and copies ran while one was open for 11% of the time, Pallas kernels for 0%

commit v1 on v0

--- a/solution.py
+++ b/solution.py
@@ -64,7 +64,17 @@
     meansq = jnp.mean(attended * attended, axis=-1, keepdims=True)
     normed = attended * lax.rsqrt(meansq + 1e-06) * head_gain.reshape(heads, DH)
     normed = normed.astype(jnp.bfloat16).reshape(tokens_here, width)
-    full_weight = lax.all_gather(out_weight, "seq", axis=1, tiled=True)
+    current_value, near = (lax.psum(1, axis_name="seq"), lax.axis_index("seq"))
+    full_weight, x_new = (out_weight, 1)
+    while x_new < current_value:
+        crops = []
+        for tick in range(current_value):
+            crops.append((tick, tick ^ x_new))
+        vec_out = lax.ppermute(full_weight, "seq", crops)
+        g_now = jnp.concatenate([full_weight, vec_out], axis=1)
+        answer = jnp.concatenate([vec_out, full_weight], axis=1)
+        full_weight = jnp.where(near & x_new == 0, g_now, answer)
+        x_new = 2 * x_new
     summed = lax.psum_scatter(
         jnp.dot(normed, full_weight, preferred_element_type=jnp.float32).astype(jnp.bfloat16),
         "hx",

time: 734 us -> 984 us (1.34)
  waiting for transfers between devices: 570 us -> 783 us
  other arithmetic: 32.9 us -> 57.4 us
    all_gather x1 -> x0, waiting for transfers between devices: 443 us -> none  [per_device(): full_weight = lax.all_gather(out_weight, 'seq', axis=1, tiled=True)]
    ppermute x0 -> x3, waiting for transfers between devices: none -> 389 us  [per_device(): vec_out = lax.ppermute(full_weight, 'seq', crops)]
    all_gather x1, waiting for transfers between devices: 26.7 us -> 293 us  [entering(): everything = lax.all_gather(x.astype(jnp.bfloat16), axis)]
    select_n x0 -> x2, other arithmetic: none -> 23.2 us  [per_device(): full_weight = jnp.where(near & x_new == 0, g_now, answer)]
    unnamed x26 -> x28, local copies, waits for them, and re-layouts: 22.9 us -> 22.2 us
  transfers between devices with their start and end apart: 3 -> 5, of which waited for: 3 -> 5; matrix products, arithmetic and copies ran while one was open for 11% -> 11% of each run, Pallas kernels for 0% -> 0%
where the time goes in v1:
time: 984 us; the launch traced here: 983 us
  waiting for transfers between devices  783 us (80%)
  matrix products  86.9 us (9%)
  other arithmetic  57.4 us (6%)
  local copies, waits for them, and re-layouts  34.7 us (4%)
  between operations  13.5 us (1%)
    ppermute x3, waiting for transfers between devices, per_device(): vec_out = lax.ppermute(full_weight, 'seq', crops)  389 us
    all_gather x1, waiting for transfers between devices, entering(): everything = lax.all_gather(x.astype(jnp.bfloat16), axis)  293 us
    reduce_scatter x1, waiting for transfers between devices, per_device(): lax.psum_scatter(jnp.dot(normed, full_weight, preferred_element_type=jnp....  101 us
    dot_general x1, matrix products, per_device(): jnp.dot(normed, full_weight, preferred_element_type=jnp.float32)  40.4 us
    select_n x2, other arithmetic, per_device(): full_weight = jnp.where(near & x_new == 0, g_now, answer)  23.2 us
    unnamed x28, local copies, waits for them, and re-layouts  22.2 us
    dot_general x2, matrix products, per_device(): jnp.einsum('hts,she->the', scores, v_part.astype(jnp.float32), precision=...  21.2 us
  transfers between devices with their start and end apart: 5, of which 5 were waited for; matrix products, arithmetic and copies ran while one was open for 11% of the time, Pallas kernels for 0%

profile of v1, /device:TPU:0, one launch (start us, length us, event | category | flops | bytes accessed | tf_op | source)
XLA Modules:
  0.0 982.9 jit_solution(1297650419907339148)
XLA Ops:
  6.5 0.0 all-gather.3.cloned.1.call-start
  6.5 3.0 collective-permute-start
  9.5 68.3 %collective-permute-done = bf16[2048,768]{1,0:T(8,128)(2,1)S(1)} collective-permute-done((bf16[2048,768]{1,0:T(8,128)(2,1)}, bf16[2048,768]{1,0:T(8,128)(2,1)S(1)}, u32[]{:S(2)}, u32[]{:S(2)}) %collective-permute-start) | collective-permute-done | bytes 3145760 | tf_op jit(solution)/shard_map/ppermute | solution.py:73
  77.8 7.6 maximum_select_fusion.5
  85.4 1.8 collective-permute-start.1
  87.3 6.3 copy.48
  93.6 5.4 fusion.19
  99.0 123.4 %collective-permute-done.1 = bf16[2048,1536]{1,0:T(8,128)(2,1)} collective-permute-done((bf16[2048,1536]{1,0:T(8,128)(2,1)}, bf16[2048,1536]{1,0:T(8,128)(2,1)}, u32[]{:S(2)}, u32[]{:S(2)}) %collective-permute-start.1) | collective-permute-done | bytes 6291488 | tf_op jit(solution)/shard_map/ppermute | solution.py:73
  222.4 15.6 %maximum_select_fusion.2 = bf16[2048,3072]{1,0:T(8,128)(2,1)} fusion(bf16[2048,1536]{1,0:T(8,128)(2,1)} %collective-permute-done.1, bf16[2048,1536]{1,0:T(8,128)(2,1)} %maximum_select_fusion.5, pred[]{:T(512)S(6)} %eq.10), kind=kLoop, calls=%fused_computation.13 | loop fusion | flops 56623104 | bytes 25165824 | tf_op jit(solution)/shard_map/jit(_where)/select_n | solution.py:76
  238.0 2.6 collective-permute-start.2
  240.6 0.0 copy-done.9
  240.6 1.7 fusion.32
  242.3 2.5 copy.81
  244.9 2.9 copy.80
  247.7 0.0 copy-start.3
  247.7 2.6 fusion.33
  250.4 0.0 copy-start.1
  250.4 0.0 copy-start.4
  250.4 1.3 copy-done.1
  251.7 0.7 fusion.36
  252.4 0.0 copy-start.7
  252.4 0.0 copy-done.4
  252.5 1.0 copy-done.7
  253.4 0.0 copy-done.3
  253.4 1.5 fusion.27
  254.9 0.0 all-gather.3.cloned.1.call-update
  255.0 0.2 reduce-scatter.2.cloned.1.call-start
  255.2 6.4 copy.47
  261.6 0.1 iota_compare_fusion
  261.7 4.2 fusion.15
  265.9 0.0 copy-start
  265.9 0.0 copy-start.5
  265.9 1.6 fusion.31
  267.5 1.2 copy-done
  268.7 0.6 copy-done.6
  269.3 0.0 copy-done.5
  269.3 2.4 fusion.35
  271.7 11.2 %fusion.7 = f32[16,512,128]{2,1,0:T(8,128)} fusion(bf16[512,16,128]{0,2,1:T(8,128)(2,1)} %bitcast.44, f32[16,512,512]{2,1,0:T(8,128)S(1)} %fusion.35, pred[512,512]{1,0:T(8,128)(4,1)S(1)} %iota_compare_fusion), kind=kOutput, calls=%fused_computation.9 | convolution fusion | flops 6446645248 | bytes 23330816 | tf_op jit(solution)/shard_map/hts,she->the/dot_general | solution.py:45
  282.9 7.3 bitcast_add_fusion
  290.3 0.0 copy-done.2
  290.3 0.0 copy-done.8
  290.3 2.4 fusion.34
  292.6 10.0 %fusion.24 = f32[512,16,128]{2,0,1:T(8,128)} fusion(bf16[512,16,128]{0,2,1:T(8,128)(2,1)S(1)} %bitcast.41, f32[16,512,512]{2,1,0:T(8,128)S(1)} %fusion.34, pred[512,512]{1,0:T(8,128)(4,1)S(1)} %iota_compare_fusion), kind=kOutput, calls=%fused_computation.37 | convolution fusion | flops 6446645248 | bytes 23330816 | tf_op jit(solution)/shard_map/hts,she->the/dot_general | solution.py:45
  302.6 293.4 %all-gather.3.cloned.1.call-done = bf16[128,128,128]{2,1,0:T(8,128)(2,1)} async-done(((bf16[16,128,128]{2,1,0:T(8,128)(2,1)}), bf16[128,128,128]{2,1,0:T(8,128)(2,1)}) %all-gather.3.cloned.1.call-update) | async-done | bytes 4194320 | tf_op jit(solution)/shard_map/all_gather | solution.py:11
  596.0 13.1 %while.14 = (s32[]{:T(128)}, f32[16,128,128]{2,1,0:T(8,128)S(1)}, s32[]{:T(128)}, bf16[8,16,128,128]{3,2,1,0:T(8,128)(2,1)}, s32[]{:T(128)}, /*index=5*/s32[]{:T(128)}) while((s32[]{:T(128)}, f32[16,128,128]{2,1,0:T(8,128)S(1)}, s32[]{:T(128)}, bf16[8,16,128,128]{3,2,1,0:T(8,128)(2,1)}, s32[]{:T(128)}, /*index=5*/s32[]{:T(128)}) %tuple.43), condition=%wide.region_1.2_spmd.clone, body=%wide.region_0.1_spmd.clone.sunk | while | flops 1048580 | bytes 2621533 | solution.py:19
  596.0 1.6 add_select_fusion.2
  597.7 1.6 add_select_fusion.2
  599.3 1.6 add_select_fusion.2
  600.9 1.6 add_select_fusion.2
  602.6 1.6 add_select_fusion.2
  604.2 1.6 add_select_fusion.2
  605.9 1.6 add_select_fusion.2
  607.5 1.6 add_select_fusion.2
  609.1 0.0 copy-start.11
  609.1 11.0 %multiply_reduce_fusion = (f32[1024,16]{0,1:T(8,128)S(1)}, f32[1024,16,128]{2,0,1:T(8,128)}) fusion(f32[16,128,128]{2,1,0:T(8,128)S(1)} %get-tuple-element.84, bf16[1024,16,128]{0,2,1:T(8,128)(2,1)} %bitcast.39, f32[512,16,128]{2,0,1:T(8,128)} %bitcast_add_fusion, f32[512,16,128]{2,0,1:T(8,128)} %fusion.24), kind=kOutput, calls=%fused_computation.29 | convolution fusion | flops 3229597696 | bytes 22085632 | tf_op jit(solution)/shard_map/thd,hde->the/dot_general | solution.py:61
  620.1 0.0 copy-done.11
  620.1 6.9 multiply_convert_fusion
  627.0 6.4 copy.65
  633.5 196.8 %collective-permute-done.2 = bf16[2048,3072]{1,0:T(8,128)(2,1)} collective-permute-done((bf16[2048,3072]{1,0:T(8,128)(2,1)}, bf16[2048,3072]{1,0:T(8,128)(2,1)}, u32[]{:S(2)}, u32[]{:S(2)}) %collective-permute-start.2) | collective-permute-done | bytes 12582944 | tf_op jit(solution)/shard_map/ppermute | solution.py:73
  830.3 40.4 %fusion.11 = bf16[1024,6144]{1,0:T(8,128)(2,1)} fusion(bf16[1024,2048]{0,1:T(8,128)(2,1)} %bitcast.51, bf16[2048,3072]{1,0:T(8,128)(2,1)} %collective-permute-done.2, bf16[2048,3072]{1,0:T(8,128)(2,1)} %maximum_select_fusion.2, pred[]{:T(512)S(6)} %eq.9), kind=kOutput, calls=%fused_computation.14 | convolution fusion | flops 25889341440 | bytes 41943040 | tf_op jit(solution)/shard_map/dot_general | solution.py:79
  870.7 0.0 reduce-scatter.2.cloned.1.call-update
  870.7 100.6 %reduce-scatter.2.cloned.1.call-done = bf16[256,6144]{1,0:T(8,128)(2,1)} async-done(((bf16[1024,6144]{1,0:T(8,128)(2,1)}), bf16[256,6144]{1,0:T(8,128)(2,1)}) %reduce-scatter.2.cloned.1.call-update) | async-done | bytes 3145744 | tf_op jit(solution)/shard_map/reduce_scatter | solution.py:78
  971.3 0.0 copy-done.10
  971.3 4.7 add_convert_fusion
  (7 shorter events, 0.0 us)
Async XLA Ops:
  6.5 589.5 %all-gather.3.cloned.1.call-start = ((), (), s32[]{:S(2)}) async-start(), calls=%async_computation.2 | async-start | bytes 4718592 | tf_op jit(solution)/shard_map/all_gather | solution.py:11
  6.5 71.3 %collective-permute-start = (bf16[2048,768]{1,0:T(8,128)(2,1)}, bf16[2048,768]{1,0:T(8,128)(2,1)S(1)}, u32[]{:S(2)}, u32[]{:S(2)}) collective-permute-start(bf16[2048,768]{1,0:T(8,128)(2,1)} %param.12), channel_id=1, source_target_pairs={{0,4},{4,0},{8,12},{12,8},{16,20},{20,16},{24,28},{28,24},{1,5},{5... | collective-permute-start | bytes 9437192 | tf_op jit(solution)/shard_map/ppermute | solution.py:73
  85.4 137.0 %collective-permute-start.1 = (bf16[2048,1536]{1,0:T(8,128)(2,1)}, bf16[2048,1536]{1,0:T(8,128)(2,1)}, u32[]{:S(2)}, u32[]{:S(2)}) collective-permute-start(bf16[2048,1536]{1,0:T(8,128)(2,1)} %maximum_select_fusion.5), channel_id=1, source_target_pairs={{0,8},{4,12},{8,0},{12,4},{16,24},{20,28},{24,16},{28,20},{1,9},{5... | collective-permute-start | bytes 18874376 | tf_op jit(solution)/shard_map/ppermute | solution.py:73
  99.0 141.6 %copy-start.9 = (bf16[1024,2048]{1,0:T(8,128)(2,1)S(1)}, bf16[1024,2048]{1,0:T(8,128)(2,1)}, u32[]{:S(2)}) copy-start(bf16[1024,2048]{1,0:T(8,128)(2,1)} %param.10) | copy-start | bytes 12582916
  238.0 592.3 %collective-permute-start.2 = (bf16[2048,3072]{1,0:T(8,128)(2,1)}, bf16[2048,3072]{1,0:T(8,128)(2,1)}, u32[]{:S(2)}, u32[]{:S(2)}) collective-permute-start(bf16[2048,3072]{1,0:T(8,128)(2,1)} %maximum_select_fusion.2), channel_id=1, source_target_pairs={{0,16},{4,20},{8,24},{12,28},{16,0},{20,4},{24,8},{28,12},{1,17},{... | collective-permute-start | bytes 37748744 | tf_op jit(solution)/shard_map/ppermute | solution.py:73
  247.7 5.7 copy-start.3
  250.4 1.3 copy-start.1
  250.4 2.1 copy-start.4
  252.4 1.0 copy-start.7
  255.0 716.3 %reduce-scatter.2.cloned.1.call-start = ((), (), s32[]{:S(2)}) async-start(), calls=%async_computation.1 | async-start | bytes 15728640 | tf_op jit(solution)/shard_map/reduce_scatter | solution.py:78
  265.9 2.8 copy-start
  265.9 3.4 copy-start.5
  267.5 1.8 copy-start.6
  282.9 7.3 copy-start.2
  282.9 7.4 copy-start.8
  609.1 11.0 %copy-start.11 = (f32[2048]{0:T(1024)S(1)}, f32[2048]{0:T(1024)}, u32[]{:S(2)}) copy-start(f32[2048]{0:T(1024)} %param.11) | copy-start | bytes 24580
  870.7 100.6 %copy-start.10 = (bf16[256,6144]{1,0:T(8,128)(2,1)S(1)}, bf16[256,6144]{1,0:T(8,128)(2,1)}, u32[]{:S(2)}) copy-start(bf16[256,6144]{1,0:T(8,128)(2,1)} %param.13) | copy-start | bytes 9437188
Sparse Core Ops, SparseCore 0:
  255.1 340.8 all-gather.2
  870.9 100.3 reduce-scatter.1
